TPU v7x, 512 devices: a whole 4x4x16 slice. The times are simulated.
512 devices in a mesh: band: 16 (over x, y), region: 32 (over z, core).
Axes of the slice: x: 4, y: 4, z: 16, core: 2. Of those that a mesh axis runs over, the one named last changes fastest.
Arguments:
- state: bfloat16 [16, 32768], P(None, 'region'), may hold values from -4 to 4
- absorb_weight: bfloat16 [16, 16384], P(None, 'band'), may hold values from -1.5 to 1.5
- emit_weight: bfloat16 [16, 16384], P(None, 'band'), may hold values from -1.5 to 1.5
- path_len: float32 [8, 8192], P(None, 'region'), may hold values from 0.02 to 0.2
- crossing_slot: int32 [8, 8192], P(None, 'region'), may hold values from 0 to 4095, as said below
- request_rows: int32 [32, 32, 128], P('region'), may hold values from 0 to 1023
- cot_intensity: float32 [16384, 8192], P('band', 'region'), may hold values from -6 to 6
Outputs:
- grad_state: float32 [16, 32768], P(None, 'region')
Inputs may be any that keep to these rules, and one draw needn't show every extreme that they name: `crossing_slot`: within each ray block (the 256 rays of one index of region) the 2048 crossings take distinct slots; slot p * 128 + s names the cell listed at request_rows[block, p, s]. In every draw one region has all 128 of its slots taken by every ray block; the other listed slots are partly unused.
All inputs are finite; a program needn't handle non-finite values.
Results may differ from a plain program's by a relative error of at most 0.0051.
Values may be sent and summed in bfloat16 or wider, within the bound.
No kernel may reach another device: no remote copies, remote signals or barrier semaphores. Data moves between devices by JAX's collectives and lax.ppermute only.
A program may use at most 64 MiB of HBM per device.

v0:
```python
import jax
import jax.numpy as jnp
from jax import lax
from jax.sharding import PartitionSpec as P


def adjoint_block(absorb_x, emit_x, length, cot_block, w_abs, w_emit):
    depth_step = absorb_x.astype(jnp.float32) * length[None]
    passed = jnp.cumsum(depth_step, axis=1) - depth_step
    transmit = jnp.exp(-passed)
    emitted = emit_x.astype(jnp.float32) * length[None] * transmit
    behind = lax.cumsum(emitted, axis=1, reverse=True) - emitted
    grad_emit = (cot_block[:, None, :] * emitted).astype(jnp.bfloat16)
    grad_absorb = (-cot_block[:, None, :] * depth_step * behind).astype(jnp.bfloat16)
    bin_count = grad_emit.shape[0]
    grad_emit = grad_emit.reshape(bin_count, -1)
    grad_absorb = grad_absorb.reshape(bin_count, -1)
    return jnp.dot(w_abs, grad_absorb, preferred_element_type=jnp.float32) + jnp.dot(
        w_emit, grad_emit, preferred_element_type=jnp.float32
    )


def on_device(
    state, absorb_weight, emit_weight, path_len, crossing_slot, request_rows, cot_intensity
):
    bin_count = absorb_weight.shape[1]
    state_count = state.shape[0]
    cross_len = path_len.shape[0]
    ray_count = path_len.shape[1]
    wanted = lax.all_to_all(
        request_rows, "region", split_axis=1, concat_axis=0, tiled=True
    ).reshape(-1)
    slot_ids = crossing_slot.reshape(-1)
    picked = jnp.take(state, wanted, axis=1)
    arrived = lax.all_to_all(picked, "region", split_axis=1, concat_axis=1, tiled=True)
    state_x = jnp.take(arrived, slot_ids, axis=1)
    absorb_x = jnp.exp(
        jnp.dot(absorb_weight.T, state_x, preferred_element_type=jnp.float32)
    ).astype(jnp.bfloat16)
    emit_x = jnp.exp(jnp.dot(emit_weight.T, state_x, preferred_element_type=jnp.float32)).astype(
        jnp.bfloat16
    )
    bin_block = 256
    summed = jnp.zeros((state_count, cross_len * ray_count), jnp.float32)
    for first_bin in range(0, bin_count, bin_block):
        last_bin = first_bin + bin_block
        summed = summed + adjoint_block(
            absorb_x[first_bin:last_bin].reshape(bin_block, cross_len, ray_count),
            emit_x[first_bin:last_bin].reshape(bin_block, cross_len, ray_count),
            path_len,
            cot_intensity[first_bin:last_bin],
            absorb_weight[:, first_bin:last_bin],
            emit_weight[:, first_bin:last_bin],
        )
    sending = jnp.zeros((state_count, wanted.shape[0]), jnp.float32).at[:, slot_ids].set(summed)
    returned = lax.all_to_all(sending, "region", split_axis=1, concat_axis=1, tiled=True)
    partial_value = (
        jnp.zeros((state_count, state.shape[1]), jnp.float32).at[:, wanted].add(returned)
    )
    partial_value = lax.psum(partial_value, "band")
    return partial_value


def solution(mesh):
    return jax.shard_map(
        on_device,
        mesh=mesh,
        in_specs=(
            P(None, "region"),
            P(None, "band"),
            P(None, "band"),
            P(None, "region"),
            P(None, "region"),
            P("region", None, None),
            P("band", "region"),
        ),
        out_specs=P(None, "region"),
        check_vma=False,
    )
```

profile of v0, /device:TPU:32, one launch (start us, length us, event | category | flops | bytes accessed | tf_op | source)
XLA Modules:
  0.0 268.6 jit_solution(6498890352738340585)
XLA Ops:
  6.5 15.5 %all-to-all-start = ((s32[1,32,128]{2,0,1:T(1,128)}), s32[1,32,128]{2,0,1:T(1,128)S(1)}, u32[]{:S(2)}, u32[]{:S(2)}) async-start(s32[1,32,128]{2,0,1:T(1,128)} %bitcast.180), calls=%async_computation | async-start | bytes 32768 | tf_op jit(solution)/shard_map/all_to_all | solution.py:30
  22.0 0.7 copy.52
  23.3 0.9 copy.36
  24.3 8.9 %all-to-all-done = s32[1,32,128]{2,0,1:T(1,128)S(1)} async-done(((s32[1,32,128]{2,0,1:T(1,128)}), s32[1,32,128]{2,0,1:T(1,128)S(1)}, u32[]{:S(2)}, u32[]{:S(2)}) %all-to-all-start) | async-done | bytes 16416 | tf_op jit(solution)/shard_map/all_to_all | solution.py:30
  33.8 12.1 %gather_fusion = bf16[4096,16]{1,0:T(8,128)(2,1)S(1)} fusion(bf16[16,1024]{0,1:T(8,128)(2,1)S(1)} %copy.36, s32[4096]{0:T(1024)S(1)} %broadcast_clamp_fusion), kind=kCustom, calls=%fused_computation | custom fusion | bytes 278528 | tf_op jit(solution)/shard_map/jit(_take)/gather | solution.py:34
  47.0 5.0 %all-to-all-start.1 = ((bf16[16,32,128]{2,0,1:T(8,128)(2,1)}), bf16[16,32,128]{2,0,1:T(8,128)(2,1)S(1)}, u32[]{:S(2)}, u32[]{:S(2)}) async-start(bf16[16,32,128]{2,0,1:T(8,128)(2,1)} %broadcast_select_fusion.3), calls=%async_computation.1 | async-start | bytes 262144 | tf_op jit(solution)/shard_map/all_to_all | solution.py:35
  53.2 0.8 copy.43
  55.2 12.8 %all-to-all-done.1 = bf16[16,32,128]{2,0,1:T(8,128)(2,1)S(1)} async-done(((bf16[16,32,128]{2,0,1:T(8,128)(2,1)}), bf16[16,32,128]{2,0,1:T(8,128)(2,1)S(1)}, u32[]{:S(2)}, u32[]{:S(2)}) %all-to-all-start.1) | async-done | bytes 131104 | tf_op jit(solution)/shard_map/all_to_all | solution.py:35
  68.6 7.3 %gather_fusion.1 = bf16[2048,16]{1,0:T(8,128)(2,1)S(1)} fusion(bf16[16,4096]{0,1:T(8,128)(2,1)S(1)} %bitcast.166, s32[2048]{0:T(1024)} %broadcast_clamp_fusion.1), kind=kCustom, calls=%fused_computation.1 | custom fusion | bytes 139264 | tf_op jit(solution)/shard_map/jit(_take)/gather | solution.py:36
  75.9 2.4 fusion
  78.4 1.6 fusion.1
  80.0 0.7 slice_convert_fusion
  80.7 0.7 slice_convert_fusion.1
  82.1 0.9 fusion.35
  83.0 0.9 fusion.29
  84.0 2.5 fusion.5
  88.0 0.9 fusion.41
  89.0 0.9 fusion.47
  89.8 2.6 fusion.17
  95.2 6.2 %scatter_custom_fusion = f32[16,4096]{0,1:T(8,128)S(1)} fusion(s32[2048]{0:T(1024)} %bitcast.177, f32[2048,16]{1,0:T(8,128)S(1)} %copy.46, f32[]{:T(128)} %constant.41.clone.1), kind=kCustom, calls=%fused_computation.107 | custom fusion | bytes 262656 | tf_op jit(solution)/shard_map/scatter | solution.py:55
  102.0 25.2 %all_to_all.30 = f32[16,32,128]{2,0,1:T(8,128)S(1)} all-to-all(f32[16,32,128]{2,0,1:T(8,128)S(1)} %copy.47), channel_id=1, replica_groups=mesh['band'=16,'region'=32] {'region'}, dimensions={1} | all-to-all | bytes 524288 | tf_op jit(solution)/shard_map/all_to_all | solution.py:56
  127.8 23.3 %scatter_custom_fusion.1 = f32[16,1024]{0,1:T(8,128)} fusion(s32[4096]{0:T(1024)} %bitcast.173, f32[4096,16]{1,0:T(8,128)S(1)} %copy.49, f32[]{:T(128)} %constant.41.clone.1), kind=kCustom, calls=%fused_computation.111 | custom fusion | flops 65536 | bytes 66048 | tf_op jit(solution)/shard_map/scatter-add | solution.py:58
  151.0 108.9 %all-reduce.2.cloned.1.call-done = f32[16,1024]{0,1:T(8,128)} async-done(((f32[16,1024]{0,1:T(8,128)}), f32[16,1024]{0,1:T(8,128)}) %all-reduce.2.cloned.1.call-update) | async-done | bytes 65552 | tf_op jit(solution)/shard_map/psum | solution.py:60
  259.9 1.8 copy.50
  (55 shorter events, 11.1 us)
Async XLA Ops:
  6.5 45.5 %copy-start.1 = (f32[1024,256]{1,0:T(8,128)S(1)}, f32[1024,256]{1,0:T(8,128)}, u32[]{:S(2)}) copy-start(f32[1024,256]{1,0:T(8,128)} %param.13) | copy-start | bytes 3145732
  6.5 26.7 %all-to-all-start = ((s32[1,32,128]{2,0,1:T(1,128)}), s32[1,32,128]{2,0,1:T(1,128)S(1)}, u32[]{:S(2)}, u32[]{:S(2)}) async-start(s32[1,32,128]{2,0,1:T(1,128)} %bitcast.180), calls=%async_computation | async-start | bytes 32768 | tf_op jit(solution)/shard_map/all_to_all | solution.py:30
  33.2 0.6 copy-start.5
  46.3 5.9 %copy-start.2 = (f32[8,256]{1,0:T(8,128)S(1)}, f32[8,256]{1,0:T(8,128)}, u32[]{:S(2)}) copy-start(f32[8,256]{1,0:T(8,128)} %param.10) | copy-start | bytes 24580
  46.3 5.9 %copy-start.6 = (s32[8,256]{1,0:T(8,128)S(1)}, s32[8,256]{1,0:T(8,128)}, u32[]{:S(2)}) copy-start(s32[8,256]{1,0:T(8,128)} %param.11) | copy-start | bytes 24580
  47.0 21.1 %all-to-all-start.1 = ((bf16[16,32,128]{2,0,1:T(8,128)(2,1)}), bf16[16,32,128]{2,0,1:T(8,128)(2,1)S(1)}, u32[]{:S(2)}, u32[]{:S(2)}) async-start(bf16[16,32,128]{2,0,1:T(8,128)(2,1)} %broadcast_select_fusion.3), calls=%async_computation.1 | async-start | bytes 262144 | tf_op jit(solution)/shard_map/all_to_all | solution.py:35
  52.0 207.9 %all-reduce.2.cloned.1.call-start = ((), (), s32[]{:S(2)}) async-start(), calls=%async_computation.3 | async-start | bytes 1048576 | tf_op jit(solution)/shard_map/psum | solution.py:60
  52.3 2.4 copy-start.7
  75.9 2.4 copy-start.4
  75.9 2.4 copy-start.8
  83.0 1.0 copy-start
  84.0 2.6 copy-start.3
Sparse Core Ops, SparseCore 0:
  151.2 108.6 all-reduce.1
where the time goes:
time: 269 us
  waiting for transfers between devices  131 us (49%)
  other arithmetic  37.5 us (14%)
  local copies, waits for them, and re-layouts  33.9 us (13%)
  blocking collectives  25.2 us (9%)
  starting transfers between devices  20.5 us (8%)
  between operations  13.8 us (5%)
  matrix products  7.06 us (3%)
    psum x1, waiting for transfers between devices, on_device(): partial_value = lax.psum(partial_value, 'band')  109 us
    all_to_all x1, blocking collectives, on_device(): lax.all_to_all(sending, 'region', split_axis=1, concat_axis=1, tiled=True)  25.2 us
    scatter-add x1, other arithmetic, on_device(): jnp.zeros((state_count, state.shape[1]), jnp.float32).at[:, wanted]  23.3 us
    all_to_all x1, starting transfers between devices, on_device(): lax.all_to_all(request_rows, 'region', split_axis=1, concat_axis=0, tiled...  15.5 us
    all_to_all x1, waiting for transfers between devices, on_device(): lax.all_to_all(picked, 'region', split_axis=1, concat_axis=1, tiled=True)  12.8 us
    gather x2, local copies, waits for them, and re-layouts, on_device(): picked = jnp.take(state, wanted, axis=1)  12.5 us
    all_to_all x1, waiting for transfers between devices, on_device(): lax.all_to_all(request_rows, 'region', split_axis=1, concat_axis=0, tiled...  8.92 us
    gather x1, local copies, waits for them, and re-layouts, on_device(): state_x = jnp.take(arrived, slot_ids, axis=1)  7.34 us
  transfers between devices with their start and end apart: 3, of which 3 were waited for; matrix products, arithmetic and copies ran while one was open for 2% of the time, Pallas kernels for 0%

commit v1 on v0

--- a/solution.py
+++ b/solution.py
@@ -2,6 +2,7 @@
 import jax.numpy as jnp
 from jax import lax
 from jax.sharding import PartitionSpec as P
+from jax.lax import all_to_all, axis_size
 
 
 def adjoint_block(absorb_x, emit_x, length, cot_block, w_abs, w_emit):
@@ -32,7 +33,10 @@
     ).reshape(-1)
     slot_ids = crossing_slot.reshape(-1)
     picked = jnp.take(state, wanted, axis=1)
-    arrived = lax.all_to_all(picked, "region", split_axis=1, concat_axis=1, tiled=True)
+    arrived = jnp.concatenate(
+        all_to_all(jnp.stack(jnp.split(picked, axis_size("region"), axis=1)), "region", 0, 0),
+        axis=1,
+    )
     state_x = jnp.take(arrived, slot_ids, axis=1)
     absorb_x = jnp.exp(
         jnp.dot(absorb_weight.T, state_x, preferred_element_type=jnp.float32)

time: 269 us -> 292 us (1.086)
  local copies, waits for them, and re-layouts: 33.9 us -> 55.3 us
    unnamed x22 -> x53, local copies, waits for them, and re-layouts: 2.32 us -> 20.7 us
    another operation x0 -> x35, local copies, waits for them, and re-layouts: none -> 3.35 us  [on_device(): jnp.stack(jnp.split(picked, axis_size('region'), axis=1))]
    gather x2 -> x1, local copies, waits for them, and re-layouts: 12.5 us -> 12.1 us  [on_device(): picked = jnp.take(state, wanted, axis=1)]
where the time goes in v1:
time: 292 us; the launch traced here: 291 us
  waiting for transfers between devices  131 us (45%)
  local copies, waits for them, and re-layouts  55.3 us (19%)
  other arithmetic  39 us (13%)
  blocking collectives  25.2 us (9%)
  starting transfers between devices  20.4 us (7%)
  between operations  13.8 us (5%)
  matrix products  7.07 us (2%)
    psum x1, waiting for transfers between devices, on_device(): partial_value = lax.psum(partial_value, 'band')  109 us
    all_to_all x1, blocking collectives, on_device(): lax.all_to_all(sending, 'region', split_axis=1, concat_axis=1, tiled=True)  25.2 us
    scatter-add x1, other arithmetic, on_device(): jnp.zeros((state_count, state.shape[1]), jnp.float32).at[:, wanted]  23.3 us
    unnamed x53, local copies, waits for them, and re-layouts  20.7 us
    all_to_all x1, starting transfers between devices, on_device(): lax.all_to_all(request_rows, 'region', split_axis=1, concat_axis=0, tiled...  15.4 us
    all_to_all x1, waiting for transfers between devices, on_device(): all_to_all(jnp.stack(jnp.split(picked, axis_size('region'), axis=1)), 're...  12.8 us
    gather x1, local copies, waits for them, and re-layouts, on_device(): picked = jnp.take(state, wanted, axis=1)  12.1 us
    all_to_all x1, waiting for transfers between devices, on_device(): lax.all_to_all(request_rows, 'region', split_axis=1, concat_axis=0, tiled...  8.92 us
  transfers between devices with their start and end apart: 3, of which 3 were waited for; matrix products, arithmetic and copies ran while one was open for 2% of the time, Pallas kernels for 0%

profile of v1, /device:TPU:32, one launch (start us, length us, event | category | flops | bytes accessed | tf_op | source)
XLA Modules:
  0.0 291.3 jit_solution(16854786309509785310)
XLA Ops:
  6.5 15.4 %all-to-all-start = ((s32[1,32,128]{2,0,1:T(1,128)}), s32[1,32,128]{2,0,1:T(1,128)S(1)}, u32[]{:S(2)}, u32[]{:S(2)}) async-start(s32[1,32,128]{2,0,1:T(1,128)} %bitcast.244), calls=%async_computation | async-start | bytes 32768 | tf_op jit(solution)/shard_map/all_to_all | solution.py:31
  21.9 0.7 copy.114
  23.2 0.9 copy.67
  24.1 8.9 %all-to-all-done = s32[1,32,128]{2,0,1:T(1,128)S(1)} async-done(((s32[1,32,128]{2,0,1:T(1,128)}), s32[1,32,128]{2,0,1:T(1,128)S(1)}, u32[]{:S(2)}, u32[]{:S(2)}) %all-to-all-start) | async-done | bytes 16416 | tf_op jit(solution)/shard_map/all_to_all | solution.py:31
  33.7 12.1 %gather_fusion = bf16[4096,16]{1,0:T(8,128)(2,1)S(1)} fusion(bf16[16,1024]{0,1:T(8,128)(2,1)S(1)} %copy.67, s32[4096]{0:T(1024)S(1)} %broadcast_clamp_fusion), kind=kCustom, calls=%fused_computation | custom fusion | bytes 278528 | tf_op jit(solution)/shard_map/jit(_take)/gather | solution.py:35
  45.8 2.1 select_bitcast_fusion
  69.8 5.0 %all-to-all-start.1 = ((bf16[32,16,128]{2,1,0:T(8,128)(2,1)}), bf16[32,16,128]{2,1,0:T(8,128)(2,1)S(1)}, u32[]{:S(2)}, u32[]{:S(2)}) async-start(bf16[32,16,128]{2,1,0:T(8,128)(2,1)} %constant_dynamic-update-slice_fusion), calls=%async_computation.1 | async-start | bytes 262144 | tf_op jit(solution)/shard_map/all_to_all | solution.py:37
  76.0 0.8 copy.105
  78.0 12.8 %all-to-all-done.1 = bf16[32,16,128]{2,1,0:T(8,128)(2,1)S(1)} async-done(((bf16[32,16,128]{2,1,0:T(8,128)(2,1)}), bf16[32,16,128]{2,1,0:T(8,128)(2,1)S(1)}, u32[]{:S(2)}, u32[]{:S(2)}) %all-to-all-start.1) | async-done | bytes 131104 | tf_op jit(solution)/shard_map/all_to_all | solution.py:37
  91.3 7.3 %gather_fusion.1 = bf16[2048,16]{1,0:T(8,128)(2,1)S(1)} fusion(bf16[16,4096]{0,1:T(8,128)(2,1)S(1)} %bitcast.230, s32[2048]{0:T(1024)} %broadcast_clamp_fusion.1), kind=kCustom, calls=%fused_computation.1 | custom fusion | bytes 139264 | tf_op jit(solution)/shard_map/jit(_take)/gather | solution.py:40
  98.7 2.4 fusion
  101.1 1.6 fusion.1
  102.7 0.7 slice_convert_fusion
  104.8 0.9 fusion.35
  105.8 0.9 fusion.29
  106.7 2.5 fusion.5
  110.8 0.9 fusion.41
  111.7 0.9 fusion.47
  112.6 2.6 fusion.17
  117.9 6.2 %scatter_custom_fusion = f32[16,4096]{0,1:T(8,128)S(1)} fusion(s32[2048]{0:T(1024)} %bitcast.241, f32[2048,16]{1,0:T(8,128)S(1)} %copy.108, f32[]{:T(128)} %constant.41.clone.1), kind=kCustom, calls=%fused_computation.108 | custom fusion | bytes 262656 | tf_op jit(solution)/shard_map/scatter | solution.py:59
  124.7 25.2 %all_to_all.26 = f32[16,32,128]{2,0,1:T(8,128)S(1)} all-to-all(f32[16,32,128]{2,0,1:T(8,128)S(1)} %copy.109), channel_id=1, replica_groups=mesh['band'=16,'region'=32] {'region'}, dimensions={1} | all-to-all | bytes 524288 | tf_op jit(solution)/shard_map/all_to_all | solution.py:60
  150.5 23.3 %scatter_custom_fusion.1 = f32[16,1024]{0,1:T(8,128)} fusion(s32[4096]{0:T(1024)} %bitcast.237, f32[4096,16]{1,0:T(8,128)S(1)} %copy.111, f32[]{:T(128)} %constant.41.clone.1), kind=kCustom, calls=%fused_computation.112 | custom fusion | flops 65536 | bytes 66048 | tf_op jit(solution)/shard_map/scatter-add | solution.py:62
  173.8 108.9 %all-reduce.2.cloned.1.call-done = f32[16,1024]{0,1:T(8,128)} async-done(((f32[16,1024]{0,1:T(8,128)}), f32[16,1024]{0,1:T(8,128)}) %all-reduce.2.cloned.1.call-update) | async-done | bytes 65552 | tf_op jit(solution)/shard_map/psum | solution.py:64
  282.7 1.8 copy.112
  (120 shorter events, 32.5 us)
Async XLA Ops:
  6.5 26.5 %all-to-all-start = ((s32[1,32,128]{2,0,1:T(1,128)}), s32[1,32,128]{2,0,1:T(1,128)S(1)}, u32[]{:S(2)}, u32[]{:S(2)}) async-start(s32[1,32,128]{2,0,1:T(1,128)} %bitcast.244), calls=%async_computation | async-start | bytes 32768 | tf_op jit(solution)/shard_map/all_to_all | solution.py:31
  33.1 0.6 copy-start.5
  48.0 26.8 %copy-start.1 = (f32[1024,256]{1,0:T(8,128)S(1)}, f32[1024,256]{1,0:T(8,128)}, u32[]{:S(2)}) copy-start(f32[1024,256]{1,0:T(8,128)} %param.13) | copy-start | bytes 3145732
  49.7 25.3 %copy-start.2 = (f32[8,256]{1,0:T(8,128)S(1)}, f32[8,256]{1,0:T(8,128)}, u32[]{:S(2)}) copy-start(f32[8,256]{1,0:T(8,128)} %param.10) | copy-start | bytes 24580
  49.7 25.3 %copy-start.6 = (s32[8,256]{1,0:T(8,128)S(1)}, s32[8,256]{1,0:T(8,128)}, u32[]{:S(2)}) copy-start(s32[8,256]{1,0:T(8,128)} %param.11) | copy-start | bytes 24580
  69.8 21.1 %all-to-all-start.1 = ((bf16[32,16,128]{2,1,0:T(8,128)(2,1)}), bf16[32,16,128]{2,1,0:T(8,128)(2,1)S(1)}, u32[]{:S(2)}, u32[]{:S(2)}) async-start(bf16[32,16,128]{2,1,0:T(8,128)(2,1)} %constant_dynamic-update-slice_fusion), calls=%async_computation.1 | async-start | bytes 262144 | tf_op jit(solution)/shard_map/all_to_all | solution.py:37
  74.7 207.9 %all-reduce.2.cloned.1.call-start = ((), (), s32[]{:S(2)}) async-start(), calls=%async_computation.3 | async-start | bytes 1048576 | tf_op jit(solution)/shard_map/psum | solution.py:64
  75.0 2.4 copy-start.7
  98.7 2.4 copy-start.4
  98.7 2.4 copy-start.8
  105.8 1.0 copy-start
  106.7 2.6 copy-start.3
Sparse Core Ops, SparseCore 0:
  173.9 108.6 all-reduce.1
